TPU v7x, 512 devices: a whole 4x4x16 slice. The times are simulated.
512 devices in a mesh: wide: 64 (over z, x), narrow: 8 (over y, core).
Axes of the slice: x: 4, y: 4, z: 16, core: 2. Of those that a mesh axis runs over, the one named last changes fastest.
Arguments:
- hidden: bfloat16 [2048, 8192], P('wide', 'narrow'), may hold values from -6 to 6
- norm_gain: float32 [8192], P('narrow'), may hold values from 0.1 to 1.9
- head_weight: bfloat16 [8192, 32000], P('narrow', 'wide'), may hold values from -0.24 to 0.24
- diff_rows: bfloat16 [64, 8, 8, 32000], P('wide', 'narrow'), may hold values from -6 to 480
- slot_request: int32 [64, 8, 8], replicated, may hold values from 0 to 2047, as said below
- slot_code: int32 [64, 8, 8], replicated, may hold values from 1 to 8
- slot_count: int32 [64, 8], replicated, may hold values from 1 to 8, as said below
Outputs:
- log_probs: float32 [2048, 32000], P('narrow', 'wide')
Inputs may be any that keep to these rules, and one draw needn't show every extreme that they name: `slot_request`: within one pair, every request is named at most once. `slot_count`: slots at or beyond the count hold no row to use; in every draw some device uses all 8 slots.
All inputs are finite; a program needn't handle non-finite values.
Results may differ from a plain program's by a relative error of at most 0.0003.
Values may be sent and summed in bfloat16 or wider, within the bound.
A program may use at most 64 MiB of HBM per device.

v0:
```python
import jax
import jax.numpy as jnp
from jax import lax
from jax.sharding import PartitionSpec as P

D = 8192
epsilon = 1e-05


def combined_all(part, axis, combine):
    gathered = jax.tree.map(lambda a: lax.all_gather(a, axis), part)

    def take(source):
        return jax.tree.map(lambda a: lax.dynamic_index_in_dim(a, source, 0, False), gathered)

    return lax.fori_loop(
        1, lax.axis_size(axis), lambda source, state: combine(state, take(source)), take(0)
    )


def merge_pair(earlier, later):
    row_peak = jnp.maximum(earlier[0], later[0])
    summed = earlier[1] * jnp.exp(earlier[0] - row_peak) + later[1] * jnp.exp(later[0] - row_peak)
    return (row_peak, summed)


def body(hidden, norm_gain, head_weight, diff_rows, slot_request, slot_code, slot_count):
    values = hidden.astype(jnp.float32)
    squares = lax.psum(jnp.sum(values * values, axis=1), "narrow")
    scales = lax.rsqrt(squares / D + epsilon)
    normed = (values * scales[:, None] * norm_gain[None, :]).astype(jnp.bfloat16)
    partial_value = jnp.dot(
        lax.all_gather(normed, "wide", axis=0, tiled=True),
        head_weight,
        preferred_element_type=jnp.float32,
    )
    row_block = diff_rows[0, 0]
    arrived = lax.all_to_all(row_block, "wide", split_axis=1, concat_axis=0, tiled=True)
    slot_total = row_block.shape[0]
    active = jnp.arange(slot_total, dtype=jnp.int32)[None, None, :] < slot_count[:, :, None]
    weights = jnp.where(active, slot_code, 0).astype(jnp.float32) * 0.25
    base_block = lax.psum_scatter(partial_value, "narrow", scatter_dimension=0, tiled=True)
    owner_slices = lax.all_gather(arrived, "narrow", axis=0, tiled=True)
    targets = jnp.transpose(slot_request, (1, 0, 2)).reshape(-1)
    factor_all = jnp.transpose(weights, (1, 0, 2)).reshape(-1)
    block_rows = base_block.shape[0]
    offsets = targets - lax.axis_index("narrow") * block_rows
    owned = (offsets >= 0) & (offsets < block_rows)
    factors = jnp.where(owned, factor_all, 0.0)
    target_rows = jnp.where(owned, offsets, 0)
    own_block = base_block.at[target_rows].add(owner_slices.astype(jnp.float32) * factors[:, None])
    local_peak = jnp.max(own_block, axis=1)
    local_mass = jnp.sum(jnp.exp(own_block - local_peak[:, None]), axis=1)
    row_peak, row_mass = combined_all((local_peak, local_mass), "wide", merge_pair)
    log_total = row_peak + jnp.log(row_mass)
    return own_block - log_total[:, None]


def solution(mesh):
    placed = (
        P("wide", "narrow"),
        P("narrow"),
        P("narrow", "wide"),
        P("wide", "narrow", None, None),
        P(),
        P(),
        P(),
    )
    return jax.shard_map(
        body, mesh=mesh, in_specs=placed, out_specs=P("narrow", "wide"), check_vma=False
    )
```

profile of v0, /device:TPU:32, one launch (start us, length us, event | category | flops | bytes accessed | tf_op | source)
XLA Modules:
  0.0 463.4 jit_solution(9681761703783635985)
XLA Ops:
  6.5 0.0 copy-start
  6.5 0.0 all-gather.7.cloned.1.call-start
  6.5 1.0 fusion.4
  7.6 14.9 %psum.7 = f32[32]{0:T(128)S(1)} all-reduce(f32[32]{0:T(128)S(1)} %fusion.4), channel_id=1, replica_groups=mesh['wide'=64,'narrow'=8] {'narrow'}, use_global_device_ids=true, to_apply=%region_1.0 | all-reduce | flops 32 | bytes 256 | tf_op jit(solution)/shard_map/psum | solution.py:29
  22.5 1.6 fusion.6
  24.0 0.0 all-gather.7.cloned.1.call-update
  24.0 0.0 reduce-scatter.2.cloned.1.call-start
  24.1 147.9 %all-gather.7.cloned.1.call-done = bf16[2048,1024]{1,0:T(8,128)(2,1)} async-done(((bf16[32,1024]{1,0:T(8,128)(2,1)}), bf16[2048,1024]{1,0:T(8,128)(2,1)}) %all-gather.7.cloned.1.call-update) | async-done | bytes 4194320 | tf_op jit(solution)/shard_map/all_gather | solution.py:33
  172.0 0.0 copy-done
  172.0 6.5 %fusion.7 = f32[2048,500]{0,1:T(8,128)} fusion(bf16[2048,1024]{1,0:T(8,128)(2,1)} %all-gather.7.cloned.1.call-done, bf16[1024,500]{0,1:T(8,128)(2,1)S(1)} %copy-done), kind=kOutput, calls=%fused_computation.24 | convolution fusion | flops 2097152000 | bytes 9314304 | tf_op jit(solution)/shard_map/dot_general | solution.py:32
  178.5 0.0 copy-start.1
  178.5 0.0 copy-start.2
  178.5 0.0 copy-start.3
  178.5 0.0 copy-start.4
  178.5 0.0 reduce-scatter.2.cloned.1.call-update
  178.5 0.0 all-gather.9.cloned.1.call-start
  178.6 1.0 copy-done.1
  179.5 1.1 all_to_all.14
  180.7 0.3 copy.20
  181.0 32.8 %all_to_all.19 = bf16[8,64,500]{2,0,1:T(8,128)(2,1)} all-to-all(bf16[8,64,500]{2,0,1:T(8,128)(2,1)S(1)} %copy.20), channel_id=1, replica_groups=mesh['wide'=64,'narrow'=8] {'wide'}, dimensions={1} | all-to-all | bytes 1024000 | tf_op jit(solution)/shard_map/all_to_all | solution.py:38
  213.8 0.0 all-gather.9.cloned.1.call-update
  213.8 0.0 copy-done.2
  213.8 0.1 copy.19
  214.0 0.2 sub.63
  214.1 0.0 copy-done.3
  214.2 0.0 copy-done.4
  214.2 0.1 copy.21
  214.3 0.2 select_n.54
  214.5 5.4 %reduce-scatter.2.cloned.1.call-done = f32[256,500]{0,1:T(8,128)} async-done(((f32[2048,500]{0,1:T(8,128)}), f32[256,500]{0,1:T(8,128)}) %reduce-scatter.2.cloned.1.call-update) | async-done | bytes 512016 | tf_op jit(solution)/shard_map/reduce_scatter | solution.py:42
  219.9 1.2 copy.22
  221.1 39.4 %all-gather.9.cloned.1.call-done = bf16[4096,500]{1,0:T(8,128)(2,1)} async-done(((bf16[512,500]{1,0:T(8,128)(2,1)}), bf16[4096,500]{1,0:T(8,128)(2,1)}) %all-gather.9.cloned.1.call-update) | async-done | bytes 4096016 | tf_op jit(solution)/shard_map/all_gather | solution.py:43
  260.5 28.5 %scatter_custom_fusion = f32[256,500]{1,0:T(8,128)S(1)} fusion(f32[256,500]{1,0:T(8,128)S(1)} %copy.22, s32[4096]{0:T(1024)S(1)} %bitcast.35, bf16[4096,500]{1,0:T(8,128)(2,1)} %all-gather.9.cloned.1.call-done, f32[4096]{0:T(1024)S(1)} %select_n.54), kind=kCustom, calls=%fused_computation.4 | custom fusion | flops 6144000 | bytes 4624384 | tf_op jit(solution)/shard_map/scatter-add | solution.py:51
  288.9 0.2 copy.23
  289.1 0.1 reduce_max.9
  289.3 0.2 exponential_reduce_fusion
  289.5 82.5 %all-gather.2 = f32[64,1,256]{2,1,0:T(1,128)S(1)} all-gather(f32[1,1,256]{2,1,0:T(1,128)S(1)} %bitcast.36), channel_id=2, replica_groups=mesh['wide'=64,'narrow'=8] {'wide'}, dimensions={0}, use_global_device_ids=true | all-gather | bytes 66560 | tf_op jit(solution)/shard_map/all_gather | solution.py:11
  372.0 80.4 %all-gather.3 = f32[64,1,256]{2,1,0:T(1,128)S(1)} all-gather(f32[1,1,256]{2,1,0:T(1,128)S(1)} %bitcast.37), channel_id=3, replica_groups=mesh['wide'=64,'narrow'=8] {'wide'}, dimensions={0}, use_global_device_ids=true | all-gather | bytes 66560 | tf_op jit(solution)/shard_map/all_gather | solution.py:11
  452.4 3.6 while.17
  456.1 0.8 broadcast_subtract_fusion
  (135 shorter events, 2.1 us)
Async XLA Ops:
  6.5 165.5 %copy-start = (bf16[1024,500]{0,1:T(8,128)(2,1)S(1)}, bf16[1024,500]{0,1:T(8,128)(2,1)}, u32[]{:S(2)}) copy-start(bf16[1024,500]{0,1:T(8,128)(2,1)} %param.11) | copy-start | bytes 3072004
  6.5 165.5 %all-gather.7.cloned.1.call-start = ((), (), s32[]{:S(2)}) async-start(), calls=%async_computation.2 | async-start | bytes 4259840 | tf_op jit(solution)/shard_map/all_gather | solution.py:33
  24.0 195.8 %reduce-scatter.2.cloned.1.call-start = ((), (), s32[]{:S(2)}) async-start(), calls=%async_computation.3 | async-start | bytes 4644864 | tf_op jit(solution)/shard_map/reduce_scatter | solution.py:42
  178.5 1.0 copy-start.1
  178.5 35.3 %copy-start.2 = (s32[64,8,8]{0,2,1:T(8,128)S(1)}, s32[64,8,8]{0,2,1:T(8,128)}, u32[]{:S(2)}) copy-start(s32[64,8,8]{0,2,1:T(8,128)} %param.13) | copy-start | bytes 49156
  178.5 35.7 %copy-start.3 = (s32[64,8,8]{0,2,1:T(8,128)S(1)}, s32[64,8,8]{0,2,1:T(8,128)}, u32[]{:S(2)}) copy-start(s32[64,8,8]{0,2,1:T(8,128)} %param.14) | copy-start | bytes 49156
  178.5 35.7 %copy-start.4 = (s32[64,8]{0,1:T(8,128)S(1)}, s32[64,8]{0,1:T(8,128)}, u32[]{:S(2)}) copy-start(s32[64,8]{0,1:T(8,128)} %param.15) | copy-start | bytes 6148
  178.5 82.0 %all-gather.9.cloned.1.call-start = ((), (), s32[]{:S(2)}) async-start(), calls=%async_computation.4 | async-start | bytes 4718592 | tf_op jit(solution)/shard_map/all_gather | solution.py:43
Sparse Core Ops, SparseCore 0:
  24.2 147.8 all-gather.6
  178.6 41.1 reduce-scatter.1
  222.3 38.1 all-gather.8
where the time goes:
time: 464 us; the launch traced here: 463 us
  blocking collectives  211 us (45%)
  waiting for transfers between devices  193 us (42%)
  other arithmetic  33.6 us (7%)
  between operations  13.3 us (3%)
  matrix products  6.47 us (1%)
  local copies, waits for them, and re-layouts  5.1 us (1%)
    all_gather x2, blocking collectives, combined_all(): gathered = jax.tree.map(lambda a: lax.all_gather(a, axis), part)  163 us
    all_gather x1, waiting for transfers between devices, body(): lax.all_gather(normed, 'wide', axis=0, tiled=True)  148 us
    all_gather x1, waiting for transfers between devices, body(): owner_slices = lax.all_gather(arrived, 'narrow', axis=0, tiled=True)  39.4 us
    all_to_all x1, blocking collectives, body(): lax.all_to_all(row_block, 'wide', split_axis=1, concat_axis=0, tiled=True)  32.8 us
    scatter-add x1, other arithmetic, body(): base_block.at[target_rows]  28.5 us
    psum x1, blocking collectives, body(): squares = lax.psum(jnp.sum(values * values, axis=1), 'narrow')  14.9 us
  transfers between devices with their start and end apart: 3, of which 3 were waited for; matrix products, arithmetic and copies ran while one was open for 0% of the time, Pallas kernels for 0%

commit v1 on v0

--- a/solution.py
+++ b/solution.py
@@ -30,7 +30,9 @@
     scales = lax.rsqrt(squares / D + epsilon)
     normed = (values * scales[:, None] * norm_gain[None, :]).astype(jnp.bfloat16)
     partial_value = jnp.dot(
-        lax.all_gather(normed, "wide", axis=0, tiled=True),
+        jnp.concatenate(
+            lax.all_to_all(jnp.stack([normed] * lax.axis_size("wide")), "wide", 0, 0), axis=0
+        ),
         head_weight,
         preferred_element_type=jnp.float32,
     )

time: 464 us -> 516 us (1.11)
  blocking collectives: 211 us -> 418 us
  waiting for transfers between devices: 193 us -> 39.1 us
    all_to_all x0 -> x1, blocking collectives: none -> 204 us  [body(): lax.all_to_all(jnp.stack([normed] * lax.axis_size('wide')), 'wide', 0, 0)]
    all_gather x1 -> x0, waiting for transfers between devices: 148 us -> none  [body(): lax.all_gather(normed, 'wide', axis=0, tiled=True)]
    reduce_scatter x1, waiting for transfers between devices: 5.36 us -> 0.02 us  [body(): lax.psum_scatter(partial_value, 'narrow', scatter_dimension=0, tiled=True)]
  transfers between devices with their start and end apart: 3 -> 2, of which waited for: 3 -> 1; matrix products, arithmetic and copies ran while one was open for 0% -> 0% of each run, Pallas kernels for 0% -> 0%
where the time goes in v1:
time: 516 us; the launch traced here: 515 us
  blocking collectives  418 us (81%)
  waiting for transfers between devices  39.1 us (8%)
  other arithmetic  33 us (6%)
  between operations  13.6 us (3%)
  local copies, waits for them, and re-layouts  5.62 us (1%)
    all_to_all x1, blocking collectives, body(): lax.all_to_all(jnp.stack([normed] * lax.axis_size('wide')), 'wide', 0, 0)  204 us
    all_gather x2, blocking collectives, combined_all(): gathered = jax.tree.map(lambda a: lax.all_gather(a, axis), part)  163 us
    all_gather x1, waiting for transfers between devices, body(): owner_slices = lax.all_gather(arrived, 'narrow', axis=0, tiled=True)  39 us
    all_to_all x1, blocking collectives, body(): lax.all_to_all(row_block, 'wide', split_axis=1, concat_axis=0, tiled=True)  36.3 us
    scatter-add x1, other arithmetic, body(): base_block.at[target_rows]  28.5 us
    psum x1, blocking collectives, body(): squares = lax.psum(jnp.sum(values * values, axis=1), 'narrow')  14.9 us
  transfers between devices with their start and end apart: 2, of which 1 were waited for; matrix products, arithmetic and copies ran while one was open for 0% of the time, Pallas kernels for 0%

profile of v1, /device:TPU:32, one launch (start us, length us, event | category | flops | bytes accessed | tf_op | source)
XLA Modules:
  0.0 515.5 jit_solution(10978570041285508463)
XLA Ops:
  6.5 0.0 copy-start
  6.5 0.0 reduce-scatter.2.cloned.1.call-start
  6.5 1.0 fusion.4
  7.6 14.9 %psum.7 = f32[32]{0:T(128)S(1)} all-reduce(f32[32]{0:T(128)S(1)} %fusion.4), channel_id=1, replica_groups=mesh['wide'=64,'narrow'=8] {'narrow'}, use_global_device_ids=true, to_apply=%region_1.0 | all-reduce | flops 32 | bytes 256 | tf_op jit(solution)/shard_map/psum | solution.py:29
  22.5 0.9 fusion.6
  23.4 0.5 stack.2
  23.9 204.2 %all_to_all.24 = bf16[64,32,1024]{2,1,0:T(8,128)(2,1)S(1)} all-to-all(bf16[64,32,1024]{2,1,0:T(8,128)(2,1)S(1)} %stack.2), channel_id=1, replica_groups=mesh['wide'=64,'narrow'=8] {'wide'}, dimensions={0} | all-to-all | bytes 8388608 | tf_op jit(solution)/shard_map/all_to_all | solution.py:34
  228.1 0.0 copy-done
  228.2 4.3 fusion.7
  232.5 0.0 copy-start.1
  232.5 0.0 copy-start.2
  232.5 0.0 copy-start.3
  232.5 0.0 copy-start.4
  232.5 0.0 reduce-scatter.2.cloned.1.call-update
  232.5 0.0 all-gather.6.cloned.1.call-start
  232.5 1.0 copy-done.1
  233.5 1.1 all_to_all.18
  234.6 0.3 copy.20
  234.9 36.3 %all_to_all.25 = bf16[8,64,500]{2,0,1:T(8,128)(2,1)} all-to-all(bf16[8,64,500]{2,0,1:T(8,128)(2,1)S(1)} %copy.20), channel_id=1, replica_groups=mesh['wide'=64,'narrow'=8] {'wide'}, dimensions={1} | all-to-all | bytes 1024000 | tf_op jit(solution)/shard_map/all_to_all | solution.py:40
  271.2 0.0 all-gather.6.cloned.1.call-update
  271.2 0.0 copy-done.2
  271.3 0.1 copy.19
  271.4 0.2 sub.63
  271.6 0.0 copy-done.3
  271.6 0.0 copy-done.4
  271.6 0.1 copy.21
  271.7 0.2 select_n.54
  271.9 0.0 reduce-scatter.2.cloned.1.call-done
  272.0 1.2 copy.22
  273.2 39.0 %all-gather.6.cloned.1.call-done = bf16[4096,500]{1,0:T(8,128)(2,1)} async-done(((bf16[512,500]{1,0:T(8,128)(2,1)}), bf16[4096,500]{1,0:T(8,128)(2,1)}) %all-gather.6.cloned.1.call-update) | async-done | bytes 4096016 | tf_op jit(solution)/shard_map/all_gather | solution.py:45
  312.2 28.5 %scatter_custom_fusion = f32[256,500]{1,0:T(8,128)S(1)} fusion(f32[256,500]{1,0:T(8,128)S(1)} %copy.22, s32[4096]{0:T(1024)S(1)} %bitcast.37, bf16[4096,500]{1,0:T(8,128)(2,1)} %all-gather.6.cloned.1.call-done, f32[4096]{0:T(1024)S(1)} %select_n.54), kind=kCustom, calls=%fused_computation.4 | custom fusion | flops 6144000 | bytes 4624384 | tf_op jit(solution)/shard_map/scatter-add | solution.py:53
  340.7 0.2 copy.23
  340.9 0.1 reduce_max.9
  341.0 0.2 exponential_reduce_fusion
  341.2 82.5 %all-gather.2 = f32[64,1,256]{2,1,0:T(1,128)S(1)} all-gather(f32[1,1,256]{2,1,0:T(1,128)S(1)} %bitcast.38), channel_id=2, replica_groups=mesh['wide'=64,'narrow'=8] {'wide'}, dimensions={0}, use_global_device_ids=true | all-gather | bytes 66560 | tf_op jit(solution)/shard_map/all_gather | solution.py:11
  423.7 80.4 %all-gather.3 = f32[64,1,256]{2,1,0:T(1,128)S(1)} all-gather(f32[1,1,256]{2,1,0:T(1,128)S(1)} %bitcast.39), channel_id=3, replica_groups=mesh['wide'=64,'narrow'=8] {'wide'}, dimensions={0}, use_global_device_ids=true | all-gather | bytes 66560 | tf_op jit(solution)/shard_map/all_gather | solution.py:11
  504.1 3.6 while.17
  507.8 0.8 broadcast_subtract_fusion
  (135 shorter events, 2.1 us)
Async XLA Ops:
  6.5 221.6 %copy-start = (bf16[1024,500]{0,1:T(8,128)(2,1)S(1)}, bf16[1024,500]{0,1:T(8,128)(2,1)}, u32[]{:S(2)}) copy-start(bf16[1024,500]{0,1:T(8,128)(2,1)} %param.11) | copy-start | bytes 3072004
  6.5 265.4 %reduce-scatter.2.cloned.1.call-start = ((), (), s32[]{:S(2)}) async-start(), calls=%async_computation.3 | async-start | bytes 4644864 | tf_op jit(solution)/shard_map/reduce_scatter | solution.py:44
  232.5 1.0 copy-start.1
  232.5 38.8 %copy-start.2 = (s32[64,8,8]{0,2,1:T(8,128)S(1)}, s32[64,8,8]{0,2,1:T(8,128)}, u32[]{:S(2)}) copy-start(s32[64,8,8]{0,2,1:T(8,128)} %param.13) | copy-start | bytes 49156
  232.5 39.1 %copy-start.3 = (s32[64,8,8]{0,2,1:T(8,128)S(1)}, s32[64,8,8]{0,2,1:T(8,128)}, u32[]{:S(2)}) copy-start(s32[64,8,8]{0,2,1:T(8,128)} %param.14) | copy-start | bytes 49156
  232.5 39.1 %copy-start.4 = (s32[64,8]{0,1:T(8,128)S(1)}, s32[64,8]{0,1:T(8,128)}, u32[]{:S(2)}) copy-start(s32[64,8]{0,1:T(8,128)} %param.15) | copy-start | bytes 6148
  232.5 79.7 %all-gather.6.cloned.1.call-start = ((), (), s32[]{:S(2)}) async-start(), calls=%async_computation.4 | async-start | bytes 4718592 | tf_op jit(solution)/shard_map/all_gather | solution.py:45
Sparse Core Ops, SparseCore 0:
  232.6 38.5 reduce-scatter.1
  273.6 38.5 all-gather.5

commit v2 on v0

--- a/solution.py
+++ b/solution.py
@@ -5,6 +5,14 @@
 
 D = 8192
 epsilon = 1e-05
+
+
+def tiled_gather(value, axis, dim):
+    size = lax.axis_size(axis)
+    repeats = [size if d == dim else 1 for d in range(value.ndim)]
+    return lax.all_to_all(
+        jnp.tile(value, repeats), axis, split_axis=dim, concat_axis=dim, tiled=True
+    )
 
 
 def combined_all(part, axis, combine):
@@ -40,7 +48,7 @@
     active = jnp.arange(slot_total, dtype=jnp.int32)[None, None, :] < slot_count[:, :, None]
     weights = jnp.where(active, slot_code, 0).astype(jnp.float32) * 0.25
     base_block = lax.psum_scatter(partial_value, "narrow", scatter_dimension=0, tiled=True)
-    owner_slices = lax.all_gather(arrived, "narrow", axis=0, tiled=True)
+    owner_slices = tiled_gather(arrived, "narrow", 0)
     targets = jnp.transpose(slot_request, (1, 0, 2)).reshape(-1)
     factor_all = jnp.transpose(weights, (1, 0, 2)).reshape(-1)
     block_rows = base_block.shape[0]

time: 464 us -> 492 us (1.060)
  the two profiles are of different devices: /device:TPU:32 before, /device:TPU:2 now
where the time goes in v2:
time: 492 us
  blocking collectives  209 us (42%)
  waiting for transfers between devices  195 us (40%)
  other arithmetic  44.1 us (9%)
  local copies, waits for them, and re-layouts  16.5 us (3%)
  between operations  13.6 us (3%)
  matrix products  6.45 us (1%)
    all_gather x2, blocking collectives, combined_all(): gathered = jax.tree.map(lambda a: lax.all_gather(a, axis), part)  160 us
    all_gather x1, waiting for transfers between devices, body(): lax.all_gather(normed, 'wide', axis=0, tiled=True)  147 us
    all_to_all x1, waiting for transfers between devices, tiled_gather(): lax.all_to_all(jnp.tile(value, repeats), axis, split_axis=dim, concat_axi...  48.3 us
    all_to_all x1, blocking collectives, body(): lax.all_to_all(row_block, 'wide', split_axis=1, concat_axis=0, tiled=True)  34.5 us
    scatter-add x1, other arithmetic, body(): base_block.at[target_rows]  26.6 us
    psum x1, blocking collectives, body(): squares = lax.psum(jnp.sum(values * values, axis=1), 'narrow')  14.9 us
    convert_element_type x1, local copies, waits for them, and re-layouts, body(): owner_slices.astype(jnp.float32) * factors[:, None]  9.9 us
  transfers between devices with their start and end apart: 3, of which 2 were waited for; matrix products, arithmetic and copies ran while one was open for 5% of the time, Pallas kernels for 0%

profile of v2, /device:TPU:2, one launch (start us, length us, event | category | flops | bytes accessed | tf_op | source)
XLA Modules:
  0.0 491.6 jit_solution(6794584450634103660)
XLA Ops:
  6.5 0.0 copy-start
  6.5 0.0 all-gather.6.cloned.1.call-start
  6.5 1.0 fusion
  7.6 14.9 %psum.7 = f32[32]{0:T(128)S(1)} all-reduce(f32[32]{0:T(128)S(1)} %fusion), channel_id=1, replica_groups=mesh['wide'=64,'narrow'=8] {'narrow'}, use_global_device_ids=true, to_apply=%region_1.0 | all-reduce | flops 32 | bytes 256 | tf_op jit(solution)/shard_map/psum | solution.py:37
  22.5 1.6 fusion.2
  24.0 0.0 all-gather.6.cloned.1.call-update
  24.0 0.0 copy-start.1
  24.1 0.0 reduce-scatter.2.cloned.1.call-start
  24.1 147.2 %all-gather.6.cloned.1.call-done = bf16[2048,1024]{1,0:T(8,128)(2,1)} async-done(((bf16[32,1024]{1,0:T(8,128)(2,1)}), bf16[2048,1024]{1,0:T(8,128)(2,1)}) %all-gather.6.cloned.1.call-update) | async-done | bytes 4194320 | tf_op jit(solution)/shard_map/all_gather | solution.py:41
  171.3 0.0 copy-done
  171.3 6.4 %fusion.3 = f32[2048,500]{0,1:T(8,128)} fusion(bf16[2048,1024]{1,0:T(8,128)(2,1)} %all-gather.6.cloned.1.call-done, bf16[1024,500]{0,1:T(8,128)(2,1)S(1)} %copy-done), kind=kOutput, calls=%fused_computation.22 | convolution fusion | flops 2097152000 | bytes 9314304 | tf_op jit(solution)/shard_map/dot_general | solution.py:40
  177.7 0.0 reduce-scatter.2.cloned.1.call-update
  177.7 0.0 copy-done.1
  177.8 1.1 all_to_all.16
  178.9 0.0 copy-start.2
  178.9 0.0 copy-start.3
  178.9 0.0 copy-start.4
  178.9 0.3 copy.27
  179.2 34.5 %all_to_all.22 = bf16[8,64,500]{2,0,1:T(8,128)(2,1)S(1)} all-to-all(bf16[8,64,500]{2,0,1:T(8,128)(2,1)S(1)} %copy.27), channel_id=1, replica_groups=mesh['wide'=64,'narrow'=8] {'wide'}, dimensions={1} | all-to-all | bytes 1024000 | tf_op jit(solution)/shard_map/all_to_all | solution.py:46
  213.7 0.2 copy.28
  213.9 2.2 tile.10
  216.1 4.6 all-to-all-start.1
  220.7 0.0 copy-done.2
  220.8 0.0 copy-done.3
  220.8 0.0 copy-done.4
  220.8 0.1 copy.31
  220.9 0.2 select_n.54
  221.1 0.1 copy.26
  221.2 0.2 sub.63
  221.4 48.3 %all-to-all-done.1 = bf16[8,512,500]{1,2,0:T(8,128)(2,1)} async-done(((bf16[8,512,500]{1,2,0:T(8,128)(2,1)}), bf16[8,512,500]{1,2,0:T(8,128)(2,1)}, u32[]{:S(2)}, u32[]{:S(2)}) %all-to-all-start.1) | async-done | bytes 4096032 | tf_op jit(solution)/shard_map/all_to_all | solution.py:13
  269.7 6.6 %copy_convert_fusion = f32[8,512,500]{1,0,2:T(8,128)} fusion(bf16[8,512,500]{1,2,0:T(8,128)(2,1)} %all-to-all-done.1), kind=kLoop, calls=%fused_computation.5 | loop fusion | flops 2048000 | bytes 12288000 | tf_op jit(solution)/shard_map/convert_element_type | solution.py:59
  276.3 9.9 %copy.30 = f32[8,512,500]{2,1,0:T(8,128)} copy(f32[8,512,500]{1,0,2:T(8,128)} %copy_convert_fusion) | data formatting | bytes 16384000 | tf_op jit(solution)/shard_map/convert_element_type | solution.py:59
  286.3 5.8 %bitcast_multiply_fusion = f32[4096,500]{1,0:T(8,128)} fusion(f32[8,512,500]{2,1,0:T(8,128)} %copy.30, f32[4096]{0:T(1024)S(1)} %select_n.54), kind=kLoop, calls=%fused_computation.4 | loop fusion | flops 2048000 | bytes 16400384 | tf_op jit(solution)/shard_map/mul | solution.py:59
  292.0 0.0 reduce-scatter.2.cloned.1.call-done
  292.0 1.2 copy.32
  293.3 26.6 %scatter_fusion = f32[256,500]{1,0:T(8,128)S(1)} fusion(f32[256,500]{1,0:T(8,128)S(1)} %copy.32, s32[4096]{0:T(1024)S(1)} %bitcast.35, f32[4096,500]{1,0:T(8,128)} %bitcast_multiply_fusion), kind=kCustom, calls=%fused_computation | custom fusion | flops 2048000 | bytes 24592384 | tf_op jit(solution)/shard_map/scatter-add | solution.py:59
  319.9 0.1 reduce_max.9
  320.0 0.2 exponential_reduce_fusion
  320.2 79.3 %all-gather.3 = f32[64,1,256]{2,1,0:T(1,128)S(1)} all-gather(f32[1,1,256]{2,1,0:T(1,128)S(1)} %bitcast.39), channel_id=3, replica_groups=mesh['wide'=64,'narrow'=8] {'wide'}, dimensions={0}, use_global_device_ids=true | all-gather | bytes 66560 | tf_op jit(solution)/shard_map/all_gather | solution.py:19
  399.5 80.6 %all-gather.2 = f32[64,1,256]{2,1,0:T(1,128)S(1)} all-gather(f32[1,1,256]{2,1,0:T(1,128)S(1)} %bitcast.38), channel_id=2, replica_groups=mesh['wide'=64,'narrow'=8] {'wide'}, dimensions={0}, use_global_device_ids=true | all-gather | bytes 66560 | tf_op jit(solution)/shard_map/all_gather | solution.py:19
  480.1 0.2 copy.33
  480.3 3.6 while.17
  484.0 0.8 broadcast_subtract_fusion
  (135 shorter events, 2.1 us)
Async XLA Ops:
  6.5 164.7 %copy-start = (bf16[1024,500]{0,1:T(8,128)(2,1)S(1)}, bf16[1024,500]{0,1:T(8,128)(2,1)}, u32[]{:S(2)}) copy-start(bf16[1024,500]{0,1:T(8,128)(2,1)} %param.11) | copy-start | bytes 3072004
  6.5 164.7 %all-gather.6.cloned.1.call-start = ((), (), s32[]{:S(2)}) async-start(), calls=%async_computation.3 | async-start | bytes 4259840 | tf_op jit(solution)/shard_map/all_gather | solution.py:41
  24.0 153.7 %copy-start.1 = (bf16[1,1,8,32000]{3,2,1,0:T(8,128)(2,1)S(1)}, bf16[1,1,8,32000]{3,2,1,0:T(8,128)(2,1)}, u32[]{:S(2)}) copy-start(bf16[1,1,8,32000]{3,2,1,0:T(8,128)(2,1)} %param.12) | copy-start | bytes 1536004
  24.1 268.0 %reduce-scatter.2.cloned.1.call-start = ((), (), s32[]{:S(2)}) async-start(), calls=%async_computation.4 | async-start | bytes 4644864 | tf_op jit(solution)/shard_map/reduce_scatter | solution.py:50
  178.9 41.9 %copy-start.2 = (s32[64,8,8]{0,2,1:T(8,128)S(1)}, s32[64,8,8]{0,2,1:T(8,128)}, u32[]{:S(2)}) copy-start(s32[64,8,8]{0,2,1:T(8,128)} %param.13) | copy-start | bytes 49156
  178.9 41.8 %copy-start.3 = (s32[64,8,8]{0,2,1:T(8,128)S(1)}, s32[64,8,8]{0,2,1:T(8,128)}, u32[]{:S(2)}) copy-start(s32[64,8,8]{0,2,1:T(8,128)} %param.14) | copy-start | bytes 49156
  178.9 41.8 %copy-start.4 = (s32[64,8]{0,1:T(8,128)S(1)}, s32[64,8]{0,1:T(8,128)}, u32[]{:S(2)}) copy-start(s32[64,8]{0,1:T(8,128)} %param.15) | copy-start | bytes 6148
  216.1 53.6 %all-to-all-start.1 = ((bf16[8,512,500]{1,2,0:T(8,128)(2,1)}), bf16[8,512,500]{1,2,0:T(8,128)(2,1)}, u32[]{:S(2)}, u32[]{:S(2)}) async-start(bf16[8,512,500]{1,2,0:T(8,128)(2,1)} %tile.10), calls=%async_computation.2 | async-start | bytes 8257536 | tf_op jit(solution)/shard_map/all_to_all | solution.py:13
Sparse Core Ops, SparseCore 0:
  24.2 147.0 all-gather.5
  177.9 41.8 reduce-scatter.1
